TPU v7x, 128 devices: a whole 4x4x4 slice. The times are simulated.
128 devices in a mesh: dp: 32 (over x, z, core), section: 4 (over y).
Axes of the slice: x: 4, y: 4, z: 4, core: 2. Of those that a mesh axis runs over, the one named last changes fastest.
Arguments:
- hidden: bfloat16 [12288, 4096], P('dp'), may hold values from -6 to 6
- encoded: bfloat16 [384, 128, 896], P('dp'), may hold values from -6 to 6
- owner: int32 [32, 12], P('dp'), may hold values from 0 to 5, never falling along the last dimension, each value on 1 to 4 neighbouring positions
- w_query: bfloat16 [4, 4096, 2048], P('section', 'dp'), may hold values from -0.09375 to 0.09375
- w_key: bfloat16 [4, 896, 2048], P('section'), may hold values from -0.1875 to 0.1875
- w_value: bfloat16 [4, 896, 2048], P('section'), may hold values from -0.1875 to 0.1875
- w_out: bfloat16 [4, 2048, 4096], P('section', None, 'dp'), may hold values from -0.75 to 0.75
Outputs:
- layer_outputs: bfloat16 [4, 12288, 4096], P('section', 'dp')
Inputs may be any that keep to these rules, and one draw needn't show every extreme that they name: owner[g] lists for each of dp index g's 12 neighbours the span of g it was retrieved for; the list never falls, every span owns 1 to 4 neighbours and some span exactly 4.
All inputs are finite; a program needn't handle non-finite values.
Results may differ from a plain program's by a relative error of at most 0.028.
Values may be sent and summed in bfloat16 or wider, within the bound.
No kernel may reach another device: no remote copies, remote signals or barrier semaphores. Data moves between devices by JAX's collectives and lax.ppermute only.
A program may use at most 384 MiB of HBM per device.

v0:
```python
import jax
import jax.numpy as jnp
from jax import lax
from jax.sharding import PartitionSpec as P

HEADS = 16
HDIM = 128
SPAN = 64
NBR_LEN = 128
MOST = 4
epsilon = 1e-05


def from_behind(block, axis, distance):
    devices = range(lax.axis_size(axis))
    route = [(i - distance, i) for i in devices if i - distance in devices]
    return lax.ppermute(block, axis, route)


def attend_all(query_heads, key_flat, value_flat, owners, span_ids):
    scores = jnp.einsum(
        "cthd,khd->chtk", query_heads, key_flat, preferred_element_type=jnp.float32
    ) * (1.0 / HDIM**0.5)
    belongs = jnp.repeat(owners[None, :] == span_ids[:, None], NBR_LEN, axis=1)
    weights = jnp.where(belongs[:, None, None, :], jnp.exp(scores), 0.0)
    denominator = jnp.sum(weights, axis=3, keepdims=True)
    weights_low = (weights / denominator).astype(jnp.bfloat16)
    return jnp.einsum(
        "chtk,khd->cthd", weights_low, value_flat, preferred_element_type=jnp.float32
    ).astype(jnp.bfloat16)


def prepare_keys(rows_enc, key_mat, value_mat, head_count):
    key_rows = jnp.dot(rows_enc, key_mat, preferred_element_type=jnp.float32).astype(jnp.bfloat16)
    value_rows = jnp.dot(rows_enc, value_mat, preferred_element_type=jnp.float32).astype(
        jnp.bfloat16
    )
    nbr_count = rows_enc.shape[0] // NBR_LEN
    padding = jnp.zeros((MOST, NBR_LEN, head_count, HDIM), jnp.bfloat16)
    key_blocks = jnp.concatenate(
        [key_rows.reshape(nbr_count, NBR_LEN, head_count, HDIM), padding], axis=0
    )
    value_blocks = jnp.concatenate(
        [value_rows.reshape(nbr_count, NBR_LEN, head_count, HDIM), padding], axis=0
    )
    key_flat = key_rows.reshape(nbr_count * NBR_LEN, head_count, HDIM)
    value_flat = value_rows.reshape(nbr_count * NBR_LEN, head_count, HDIM)
    return (key_blocks, value_blocks, key_flat, value_flat)


def attend(query_heads, key_pack, owners, span_ids):
    return attend_all(query_heads, key_pack[2], key_pack[3], owners, span_ids)


def per_device(hidden, encoded, owner, w_query, w_key, w_value, w_out):
    section_id = lax.axis_index("section")
    section_count = lax.axis_size("section")
    enc_width = encoded.shape[2]
    model_width = hidden.shape[1]
    rows_enc = encoded.reshape(-1, enc_width)
    owners = owner[0]
    query_full, out_full = (
        lax.all_gather(w_query, "dp", axis=1, tiled=True),
        lax.all_gather(w_out, "dp", axis=2, tiled=True),
    )
    query_mat = query_full[0]
    out_mat = out_full[0]
    own_pack = prepare_keys(rows_enc, w_key[0], w_value[0], HEADS)
    span_count = hidden.shape[0] // SPAN
    every_span = jnp.arange(span_count, dtype=jnp.int32)
    current = hidden
    stored = jnp.zeros_like(hidden)
    for step_index in range(section_count):
        if step_index > 0:
            current = from_behind(current, "section", 1)
        active = section_id == step_index
        row_count = current.shape[0]
        widened = current.astype(jnp.float32)
        normed = (
            widened * lax.rsqrt(jnp.mean(widened * widened, axis=-1, keepdims=True) + epsilon)
        ).astype(jnp.bfloat16)
        empty = jnp.zeros((row_count, model_width), jnp.float32)

        def heavy_full(operand):
            queries = jnp.dot(operand, query_mat, preferred_element_type=jnp.float32).astype(
                jnp.bfloat16
            )
            query_heads = queries.reshape(every_span.shape[0], SPAN, HEADS, HDIM)
            attended = attend(query_heads, own_pack, owners, every_span)
            return jnp.dot(
                attended.reshape(row_count, HEADS * HDIM),
                out_mat,
                preferred_element_type=jnp.float32,
            )

        def light_full(operand):
            return empty

        branch = lax.cond(active, heavy_full, light_full, normed)
        result = (widened + branch).astype(jnp.bfloat16)
        current = jnp.where(active, result, current)
        stored = jnp.where(active, result, stored)
    return stored[None]


def solution(mesh):
    placed = (
        P("dp", None),
        P("dp", None, None),
        P("dp", None),
        P("section", "dp", None),
        P("section", None, None),
        P("section", None, None),
        P("section", None, "dp"),
    )
    return jax.shard_map(
        per_device, mesh=mesh, in_specs=placed, out_specs=P("section", "dp", None), check_vma=False
    )
```

profile of v0, /device:TPU:24, one launch (start us, length us, event | category | flops | bytes accessed | tf_op | source)
XLA Modules:
  0.0 728.9 jit_solution(6954939730521494805)
XLA Ops:
  8.3 9.1 %fusion.111 = bf16[192,8,16,128]{3,1,2,0:T(8,128)(2,1)S(1)} fusion(bf16[1536,896]{1,0:T(8,128)(2,1)S(1)} %bitcast.152, bf16[1,896,2048]{2,1,0:T(8,128)(2,1)} %param.20), kind=kOutput, calls=%fused_computation.118 | convolution fusion | flops 5640290304 | bytes 12713984 | tf_op jit(solution)/shard_map/dot_general | solution.py:35
  17.4 5.0 copy.73
  22.4 7.2 fusion.108
  29.6 5.0 copy.72
  38.0 46.4 %all-gather.3.cloned.1.call-done = bf16[1,4096,2048]{2,1,0:T(8,128)(2,1)} async-done(((bf16[1,128,2048]{2,1,0:T(8,128)(2,1)}), bf16[1,4096,2048]{2,1,0:T(8,128)(2,1)}) %all-gather.3.cloned.1.call-update) | async-done | bytes 16777232 | tf_op jit(solution)/shard_map/all_gather | solution.py:63
  84.4 82.8 %all-gather.5.cloned.1.call-done = bf16[1,2048,4096]{2,1,0:T(8,128)(2,1)} async-done(((bf16[1,2048,128]{2,1,0:T(8,128)(2,1)}), bf16[1,2048,4096]{2,1,0:T(8,128)(2,1)}) %all-gather.5.cloned.1.call-update) | async-done | bytes 16777232 | tf_op jit(solution)/shard_map/all_gather | solution.py:64
  167.2 11.7 %conditional.4 = (f32[384,4096]{1,0:T(8,128)}) conditional(s32[]{:T(128)} %convert_element_type.103, () %tuple.29, (s32[1,12]{1,0:T(1,128)S(1)}, s32[6]{0:T(128)S(1)}, bf16[384,4096]{1,0:T(8,128)(2,1)}, bf16[4096,2048]{1,0:T(8,128)(2,1)}, bf16[1536,16,128]{2,1,0:T(8,128)(2,1)}, /*index=5*/bf16[1536,16,128]{2,1,0:T(8,128)(2,1)}, ...), branch_computations={%region_1.0_spmd, %region_2.4_spmd} | conditional | flops 17784367104 | bytes 143750368 | solution.py:99
  178.9 7.8 %broadcast_select_fusion = bf16[384,4096]{1,0:T(8,128)(2,1)} fusion(bf16[384,4096]{1,0:T(8,128)(2,1)} %param.15, pred[]{:T(512)S(6)} %eq.75, f32[384,4096]{1,0:T(8,128)} %get-tuple-element.165), kind=kLoop, calls=%fused_computation.114 | loop fusion | flops 6291456 | bytes 12582913 | tf_op jit(solution)/shard_map/jit(_where)/select_n | solution.py:101
  188.0 71.2 %collective-permute-done = bf16[384,4096]{1,0:T(8,128)(2,1)} collective-permute-done((bf16[384,4096]{1,0:T(8,128)(2,1)}, bf16[384,4096]{1,0:T(8,128)(2,1)}, u32[]{:S(2)}, u32[]{:S(2)}) %collective-permute-start) | collective-permute-done | bytes 3145760 | tf_op jit(solution)/shard_map/ppermute | solution.py:17
  261.8 4.6 fusion.96
  266.4 11.8 %conditional.5 = (f32[384,4096]{1,0:T(8,128)}) conditional(s32[]{:T(128)} %convert_element_type.109, () %tuple.31, (s32[1,12]{1,0:T(1,128)S(1)}, s32[6]{0:T(128)S(1)}, bf16[384,4096]{1,0:T(8,128)(2,1)}, bf16[4096,2048]{1,0:T(8,128)(2,1)}, bf16[1536,16,128]{2,1,0:T(8,128)(2,1)}, /*index=5*/bf16[1536,16,128]{2,1,0:T(8,128)(2,1)}, ...), branch_computations={%region_5.6_spmd, %region_6.8_spmd} | conditional | flops 17784367104 | bytes 143750368 | solution.py:99
  278.2 7.8 %broadcast_select_fusion.1 = bf16[384,4096]{1,0:T(8,128)(2,1)} fusion(bf16[384,4096]{1,0:T(8,128)(2,1)} %collective-permute-done, pred[]{:T(512)S(6)} %eq.74, f32[384,4096]{1,0:T(8,128)} %get-tuple-element.166), kind=kLoop, calls=%fused_computation.115 | loop fusion | flops 6291456 | bytes 12582913 | tf_op jit(solution)/shard_map/jit(_where)/select_n | solution.py:101
  287.3 70.4 %collective-permute-done.1 = bf16[384,4096]{1,0:T(8,128)(2,1)} collective-permute-done((bf16[384,4096]{1,0:T(8,128)(2,1)}, bf16[384,4096]{1,0:T(8,128)(2,1)}, u32[]{:S(2)}, u32[]{:S(2)}) %collective-permute-start.1) | collective-permute-done | bytes 3145760 | tf_op jit(solution)/shard_map/ppermute | solution.py:17
  360.2 4.6 fusion.99
  364.8 11.8 %conditional.6 = (f32[384,4096]{1,0:T(8,128)}) conditional(s32[]{:T(128)} %convert_element_type.113, () %tuple.33, (s32[1,12]{1,0:T(1,128)S(1)}, s32[6]{0:T(128)S(1)}, bf16[384,4096]{1,0:T(8,128)(2,1)}, bf16[4096,2048]{1,0:T(8,128)(2,1)}, bf16[1536,16,128]{2,1,0:T(8,128)(2,1)}, /*index=5*/bf16[1536,16,128]{2,1,0:T(8,128)(2,1)}, ...), branch_computations={%region_9.10_spmd, %region_10.12_spmd} | conditional | flops 17784367104 | bytes 143750368 | solution.py:99
  376.7 7.9 %broadcast_select_fusion.2 = bf16[384,4096]{1,0:T(8,128)(2,1)} fusion(bf16[384,4096]{1,0:T(8,128)(2,1)} %collective-permute-done.1, pred[]{:T(512)S(6)} %eq.73, f32[384,4096]{1,0:T(8,128)} %get-tuple-element.167), kind=kLoop, calls=%fused_computation.116 | loop fusion | flops 6291456 | bytes 12582913 | tf_op jit(solution)/shard_map/jit(_where)/select_n | solution.py:101
  385.9 242.9 %collective-permute-done.2 = bf16[384,4096]{1,0:T(8,128)(2,1)} collective-permute-done((bf16[384,4096]{1,0:T(8,128)(2,1)}, bf16[384,4096]{1,0:T(8,128)(2,1)}, u32[]{:S(2)}, u32[]{:S(2)}) %collective-permute-start.2) | collective-permute-done | bytes 3145760 | tf_op jit(solution)/shard_map/ppermute | solution.py:17
  631.4 4.6 fusion.102
  636.0 70.3 %conditional.7 = (f32[384,4096]{1,0:T(8,128)}) conditional(s32[]{:T(128)} %convert_element_type.117, () %tuple.35, (s32[1,12]{1,0:T(1,128)S(1)}, s32[6]{0:T(128)S(1)}, bf16[384,4096]{1,0:T(8,128)(2,1)}, bf16[4096,2048]{1,0:T(8,128)(2,1)}, bf16[1536,16,128]{2,1,0:T(8,128)(2,1)}, /*index=5*/bf16[1536,16,128]{2,1,0:T(8,128)(2,1)}, ...), branch_computations={%region_13.14_spmd, %region_14.16_spmd} | conditional | flops 17784367104 | bytes 143750368 | solution.py:99
  636.1 11.1 %fusion.84 = bf16[48,8,16,128]{3,1,2,0:T(8,128)(2,1)S(1)} fusion(bf16[384,4096]{1,0:T(8,128)(2,1)} %get-tuple-element.96, bf16[4096,2048]{1,0:T(8,128)(2,1)} %get-tuple-element.97), kind=kOutput, calls=%fused_computation.77 | convolution fusion | flops 6443237376 | bytes 21495808 | tf_op jit(solution)/shard_map/cond/branch_1_fun/dot_general | solution.py:85
  647.7 24.3 %bitcast_reduce_fusion.3 = (f32[6,16,64]{2,0,1:T(8,128)S(1)}, f32[16,6,64,1536]{3,2,1,0:T(8,128)}) fusion(pred[6,1536]{1,0:T(8,128)(4,1)S(1)} %bitcast.183, bf16[1536,16,128,1]{2,1,0,3:T(8,128)(2,1)} %bitcast.168, bf16[6,64,16,128]{3,2,1,0:T(8,128)(2,1)S(1)} %bitcast.172), kind=kOutput, calls=%fused_computation.64 | convolution fusion | flops 2444224512 | bytes 45646848 | tf_op jit(solution)/shard_map/cond/branch_1_fun/cthd,khd->chtk/dot_general | solution.py:21
  672.0 21.1 %fusion.85 = bf16[6,64,16,128]{3,1,0,2:T(8,128)(2,1)S(1)} fusion(bf16[1536,16,128,1]{2,1,0,3:T(8,128)(2,1)} %bitcast.160, f32[16,6,64,1536]{3,2,1,0:T(8,128)} %get-tuple-element.164, f32[6,16,64]{2,0,1:T(8,128)S(1)} %get-tuple-element.163, pred[6,1536]{1,0:T(8,128)(4,1)S(1)} %bitcast.184), kind=kOutput, calls=%fused_computation.78 | convolution fusion | flops 2454454272 | bytes 45646848 | tf_op jit(solution)/shard_map/cond/branch_1_fun/chtk,khd->cthd/dot_general | solution.py:28
  694.1 11.9 %fusion.80 = f32[384,4096]{1,0:T(8,128)} fusion(bf16[2048,4096]{1,0:T(8,128)(2,1)} %get-tuple-element.100, bf16[48,8,16,128]{3,2,1,0:T(8,128)(2,1)S(1)} %bitcast.176), kind=kOutput, calls=%fused_computation.73 | convolution fusion | flops 6442450944 | bytes 24641536 | tf_op jit(solution)/shard_map/cond/branch_1_fun/dot_general | solution.py:90
  706.3 15.6 %fusion.107 = bf16[1,384,4096]{2,1,0:T(8,128)(2,1)} fusion(f32[384,4096]{1,0:T(8,128)} %get-tuple-element.168, bf16[384,4096]{1,0:T(8,128)(2,1)} %collective-permute-done.2, pred[]{:T(512)S(6)} %eq.75, pred[]{:T(512)S(6)} %eq.74, pred[]{:T(512)S(6)} %eq.73, pred[]{:T(512)S(6)} %eq.72, f32[384,4096]{1,0:T(8,128)} %get-tuple-element.167, ...), kind=kLoop, calls=%fused_computation.113 | loop fusion | flops 25165824 | bytes 40894468 | tf_op jit(solution)/shard_map/broadcast_in_dim | solution.py:103
  (38 shorter events, 28.5 us)
Async XLA Ops:
  6.5 1.8 copy-start
  6.5 77.8 %all-gather.3.cloned.1.call-start = ((), (), s32[]{:S(2)}) async-start(), calls=%async_computation | async-start | bytes 17301504 | tf_op jit(solution)/shard_map/all_gather | solution.py:63
  7.3 159.9 %all-gather.5.cloned.1.call-start = ((), (), s32[]{:S(2)}) async-start(), calls=%async_computation.1 | async-start | bytes 17301504 | tf_op jit(solution)/shard_map/all_gather | solution.py:64
  17.4 5.0 copy-start.4
  29.6 5.0 copy-start.2
  34.6 132.6 %copy-start.3 = (s32[1,12]{1,0:T(1,128)S(1)}, s32[1,12]{1,0:T(1,128)}, u32[]{:S(2)}) copy-start(s32[1,12]{1,0:T(1,128)} %param.17) | copy-start | bytes 148
  186.7 72.5 %collective-permute-start = (bf16[384,4096]{1,0:T(8,128)(2,1)}, bf16[384,4096]{1,0:T(8,128)(2,1)}, u32[]{:S(2)}, u32[]{:S(2)}) collective-permute-start(bf16[384,4096]{1,0:T(8,128)(2,1)} %broadcast_select_fusion), channel_id=1, source_target_pairs={{0,1},{1,2},{2,3},{4,5},{5,6},{6,7},{8,9},{9,10},{10,11},{12,13},{... | collective-permute-start | bytes 9437192 | tf_op jit(solution)/shard_map/ppermute | solution.py:17
  286.0 71.7 %collective-permute-start.1 = (bf16[384,4096]{1,0:T(8,128)(2,1)}, bf16[384,4096]{1,0:T(8,128)(2,1)}, u32[]{:S(2)}, u32[]{:S(2)}) collective-permute-start(bf16[384,4096]{1,0:T(8,128)(2,1)} %broadcast_select_fusion.1), channel_id=1, source_target_pairs={{0,1},{1,2},{2,3},{4,5},{5,6},{6,7},{8,9},{9,10},{10,11},{12,13},{... | collective-permute-start | bytes 9437192 | tf_op jit(solution)/shard_map/ppermute | solution.py:17
  384.6 244.2 %collective-permute-start.2 = (bf16[384,4096]{1,0:T(8,128)(2,1)}, bf16[384,4096]{1,0:T(8,128)(2,1)}, u32[]{:S(2)}, u32[]{:S(2)}) collective-permute-start(bf16[384,4096]{1,0:T(8,128)(2,1)} %broadcast_select_fusion.2), channel_id=1, source_target_pairs={{0,1},{1,2},{2,3},{4,5},{5,6},{6,7},{8,9},{9,10},{10,11},{12,13},{... | collective-permute-start | bytes 9437192 | tf_op jit(solution)/shard_map/ppermute | solution.py:17
  706.2 15.6 %copy-start.1 = (bf16[12,128,896]{2,1,0:T(8,128)(2,1)S(1)}, bf16[12,128,896]{2,1,0:T(8,128)(2,1)}, u32[]{:S(2)}) copy-start(bf16[12,128,896]{2,1,0:T(8,128)(2,1)} %param.16) | copy-start | bytes 8257540
Sparse Core Ops, SparseCore 0:
  9.6 74.6 all-gather.2
  86.5 80.5 all-gather.4
where the time goes:
time: 736 us; the launch traced here: 729 us
  waiting for transfers between devices  515 us (70%)
  matrix products  84.7 us (12%)
  other arithmetic  64.1 us (9%)
  loops' own time  25.4 us (3%)
  local copies, waits for them, and re-layouts  22 us (3%)
  between operations  13.8 us (2%)
    ppermute x3, waiting for transfers between devices, from_behind(): return lax.ppermute(block, axis, route)  384 us
    all_gather x1, waiting for transfers between devices, per_device(): lax.all_gather(w_out, 'dp', axis=2, tiled=True)  82.8 us
    all_gather x1, waiting for transfers between devices, per_device(): lax.all_gather(w_query, 'dp', axis=1, tiled=True)  46.4 us
    another operation x4, loops' own time, per_device(): branch = lax.cond(active, heavy_full, light_full, normed)  25.4 us
    dot_general x1, matrix products, attend_all(): jnp.einsum('cthd,khd->chtk', query_heads, key_flat, preferred_element_typ...  24.3 us
    select_n x3, other arithmetic, per_device(): current = jnp.where(active, result, current)  23.6 us
    dot_general x1, matrix products, attend_all(): jnp.einsum('chtk,khd->cthd', weights_low, value_flat, preferred_element_t...  21.1 us
    convert_element_type x4, other arithmetic, per_device(): normed = (widened * lax.rsqrt(jnp.mean(widened * widened, axis=-1, keepdi...  16.4 us
  transfers between devices with their start and end apart: 5, of which 5 were waited for; matrix products, arithmetic and copies ran while one was open for 4% of the time, Pallas kernels for 0%

commit v1 on v0

--- a/solution.py
+++ b/solution.py
@@ -2,6 +2,7 @@
 import jax.numpy as jnp
 from jax import lax
 from jax.sharding import PartitionSpec as P
+from jax.lax import all_to_all, axis_size
 
 HEADS = 16
 HDIM = 128
@@ -60,7 +61,9 @@
     rows_enc = encoded.reshape(-1, enc_width)
     owners = owner[0]
     query_full, out_full = (
-        lax.all_gather(w_query, "dp", axis=1, tiled=True),
+        jnp.concatenate(
+            all_to_all(jnp.stack([w_query for _ in range(axis_size("dp"))]), "dp", 0, 0), axis=1
+        ),
         lax.all_gather(w_out, "dp", axis=2, tiled=True),
     )
     query_mat = query_full[0]

time: 736 us -> 872 us (1.18)
  the two profiles are of different devices: /device:TPU:24 before, /device:TPU:60 now
where the time goes in v1:
time: 872 us; the launch traced here: 865 us
  waiting for transfers between devices  637 us (73%)
  matrix products  84.8 us (10%)
  other arithmetic  64.1 us (7%)
  local copies, waits for them, and re-layouts  28.5 us (3%)
  loops' own time  25.4 us (3%)
  between operations  13.8 us (2%)
  starting transfers between devices  11.9 us (1%)
    ppermute x3, waiting for transfers between devices, from_behind(): return lax.ppermute(block, axis, route)  384 us
    all_to_all x1, waiting for transfers between devices, per_device(): all_to_all(jnp.stack([w_query for _ in range(axis_size('dp'))]), 'dp', 0, 0)  252 us
    another operation x4, loops' own time, per_device(): branch = lax.cond(active, heavy_full, light_full, normed)  25.4 us
    dot_general x1, matrix products, attend_all(): jnp.einsum('cthd,khd->chtk', query_heads, key_flat, preferred_element_typ...  24.2 us
    select_n x3, other arithmetic, per_device(): current = jnp.where(active, result, current)  23.6 us
    dot_general x1, matrix products, attend_all(): jnp.einsum('chtk,khd->cthd', weights_low, value_flat, preferred_element_t...  21.1 us
  transfers between devices with their start and end apart: 5, of which 4 were waited for; matrix products, arithmetic and copies ran while one was open for 4% of the time, Pallas kernels for 0%

profile of v1, /device:TPU:60, one launch (start us, length us, event | category | flops | bytes accessed | tf_op | source)
XLA Modules:
  0.0 865.2 jit_solution(10456389897315666247)
XLA Ops:
  7.3 6.8 stack.2
  14.1 8.0 all-to-all-start
  22.2 9.2 %fusion.111 = bf16[192,8,16,128]{3,1,2,0:T(8,128)(2,1)S(1)} fusion(bf16[1536,896]{1,0:T(8,128)(2,1)S(1)} %bitcast.153, bf16[1,896,2048]{2,1,0:T(8,128)(2,1)} %param.20), kind=kOutput, calls=%fused_computation.118 | convolution fusion | flops 5640290304 | bytes 12713984 | tf_op jit(solution)/shard_map/dot_general | solution.py:36
  31.4 5.0 copy.89
  36.4 7.2 fusion.108
  43.6 5.0 copy.88
  52.0 251.9 %all-to-all-done = bf16[32,1,128,2048]{3,2,1,0:T(8,128)(2,1)} async-done(((bf16[32,1,128,2048]{3,2,1,0:T(8,128)(2,1)}), bf16[32,1,128,2048]{3,2,1,0:T(8,128)(2,1)}, u32[]{:S(2)}, u32[]{:S(2)}) %all-to-all-start) | async-done | bytes 16777248 | tf_op jit(solution)/shard_map/all_to_all | solution.py:65
  303.8 11.7 %conditional.4 = (f32[384,4096]{1,0:T(8,128)}) conditional(s32[]{:T(128)} %convert_element_type.103, () %tuple.29, (s32[1,12]{1,0:T(1,128)S(1)}, s32[6]{0:T(128)S(1)}, bf16[384,4096]{1,0:T(8,128)(2,1)}, bf16[4096,2048]{1,0:T(8,128)(2,1)}, bf16[1536,16,128]{2,1,0:T(8,128)(2,1)}, /*index=5*/bf16[1536,16,128]{2,1,0:T(8,128)(2,1)}, ...), branch_computations={%region_1.0_spmd, %region_2.4_spmd} | conditional | flops 17784367104 | bytes 143750368 | solution.py:102
  315.6 7.8 broadcast_select_fusion
  324.7 70.8 %collective-permute-done = bf16[384,4096]{1,0:T(8,128)(2,1)} collective-permute-done((bf16[384,4096]{1,0:T(8,128)(2,1)}, bf16[384,4096]{1,0:T(8,128)(2,1)}, u32[]{:S(2)}, u32[]{:S(2)}) %collective-permute-start) | collective-permute-done | bytes 3145760 | tf_op jit(solution)/shard_map/ppermute | solution.py:18
  398.1 4.6 fusion.96
  402.7 11.8 %conditional.5 = (f32[384,4096]{1,0:T(8,128)}) conditional(s32[]{:T(128)} %convert_element_type.109, () %tuple.31, (s32[1,12]{1,0:T(1,128)S(1)}, s32[6]{0:T(128)S(1)}, bf16[384,4096]{1,0:T(8,128)(2,1)}, bf16[4096,2048]{1,0:T(8,128)(2,1)}, bf16[1536,16,128]{2,1,0:T(8,128)(2,1)}, /*index=5*/bf16[1536,16,128]{2,1,0:T(8,128)(2,1)}, ...), branch_computations={%region_5.6_spmd, %region_6.8_spmd} | conditional | flops 17784367104 | bytes 143750368 | solution.py:102
  414.5 7.8 broadcast_select_fusion.1
  423.6 70.0 %collective-permute-done.1 = bf16[384,4096]{1,0:T(8,128)(2,1)} collective-permute-done((bf16[384,4096]{1,0:T(8,128)(2,1)}, bf16[384,4096]{1,0:T(8,128)(2,1)}, u32[]{:S(2)}, u32[]{:S(2)}) %collective-permute-start.1) | collective-permute-done | bytes 3145760 | tf_op jit(solution)/shard_map/ppermute | solution.py:18
  496.2 4.6 fusion.99
  500.7 11.8 %conditional.6 = (f32[384,4096]{1,0:T(8,128)}) conditional(s32[]{:T(128)} %convert_element_type.113, () %tuple.33, (s32[1,12]{1,0:T(1,128)S(1)}, s32[6]{0:T(128)S(1)}, bf16[384,4096]{1,0:T(8,128)(2,1)}, bf16[4096,2048]{1,0:T(8,128)(2,1)}, bf16[1536,16,128]{2,1,0:T(8,128)(2,1)}, /*index=5*/bf16[1536,16,128]{2,1,0:T(8,128)(2,1)}, ...), branch_computations={%region_9.10_spmd, %region_10.12_spmd} | conditional | flops 17784367104 | bytes 143750368 | solution.py:102
  512.6 7.9 broadcast_select_fusion.2
  521.8 243.3 %collective-permute-done.2 = bf16[384,4096]{1,0:T(8,128)(2,1)} collective-permute-done((bf16[384,4096]{1,0:T(8,128)(2,1)}, bf16[384,4096]{1,0:T(8,128)(2,1)}, u32[]{:S(2)}, u32[]{:S(2)}) %collective-permute-start.2) | collective-permute-done | bytes 3145760 | tf_op jit(solution)/shard_map/ppermute | solution.py:18
  772.3 70.2 %conditional.7 = (f32[384,4096]{1,0:T(8,128)}) conditional(s32[]{:T(128)} %convert_element_type.117, () %tuple.35, (s32[1,12]{1,0:T(1,128)S(1)}, s32[6]{0:T(128)S(1)}, bf16[384,4096]{1,0:T(8,128)(2,1)}, bf16[4096,2048]{1,0:T(8,128)(2,1)}, bf16[1536,16,128]{2,1,0:T(8,128)(2,1)}, /*index=5*/bf16[1536,16,128]{2,1,0:T(8,128)(2,1)}, ...), branch_computations={%region_13.14_spmd, %region_14.16_spmd} | conditional | flops 17784367104 | bytes 143750368 | solution.py:102
  772.4 11.1 %fusion.84 = bf16[48,8,16,128]{3,1,2,0:T(8,128)(2,1)S(1)} fusion(bf16[384,4096]{1,0:T(8,128)(2,1)} %get-tuple-element.96, bf16[4096,2048]{1,0:T(8,128)(2,1)} %get-tuple-element.97), kind=kOutput, calls=%fused_computation.77 | convolution fusion | flops 6443237376 | bytes 21495808 | tf_op jit(solution)/shard_map/cond/branch_1_fun/dot_general | solution.py:88
  784.0 24.2 %bitcast_reduce_fusion.3 = (f32[6,16,64]{2,0,1:T(8,128)S(1)}, f32[16,6,64,1536]{3,2,1,0:T(8,128)}) fusion(pred[6,1536]{1,0:T(8,128)(4,1)S(1)} %bitcast.185, bf16[1536,16,128,1]{2,1,0,3:T(8,128)(2,1)} %bitcast.169, bf16[6,64,16,128]{3,2,1,0:T(8,128)(2,1)S(1)} %bitcast.173), kind=kOutput, calls=%fused_computation.64 | convolution fusion | flops 2444224512 | bytes 45646848 | tf_op jit(solution)/shard_map/cond/branch_1_fun/cthd,khd->chtk/dot_general | solution.py:22
  808.3 21.1 %fusion.85 = bf16[6,64,16,128]{3,1,0,2:T(8,128)(2,1)S(1)} fusion(bf16[1536,16,128,1]{2,1,0,3:T(8,128)(2,1)} %bitcast.161, f32[16,6,64,1536]{3,2,1,0:T(8,128)} %get-tuple-element.192, f32[6,16,64]{2,0,1:T(8,128)S(1)} %get-tuple-element.191, pred[6,1536]{1,0:T(8,128)(4,1)S(1)} %bitcast.186), kind=kOutput, calls=%fused_computation.78 | convolution fusion | flops 2454454272 | bytes 45646848 | tf_op jit(solution)/shard_map/cond/branch_1_fun/chtk,khd->cthd/dot_general | solution.py:29
  830.4 11.9 %fusion.80 = f32[384,4096]{1,0:T(8,128)} fusion(bf16[2048,4096]{1,0:T(8,128)(2,1)} %get-tuple-element.100, bf16[48,8,16,128]{3,2,1,0:T(8,128)(2,1)S(1)} %bitcast.177), kind=kOutput, calls=%fused_computation.73 | convolution fusion | flops 6442450944 | bytes 24641536 | tf_op jit(solution)/shard_map/cond/branch_1_fun/dot_general | solution.py:93
  842.5 15.6 %fusion.107 = bf16[1,384,4096]{2,1,0:T(8,128)(2,1)} fusion(f32[384,4096]{1,0:T(8,128)} %get-tuple-element.196, bf16[384,4096]{1,0:T(8,128)(2,1)} %collective-permute-done.2, pred[]{:T(512)S(6)} %eq.75, pred[]{:T(512)S(6)} %eq.74, pred[]{:T(512)S(6)} %eq.73, pred[]{:T(512)S(6)} %eq.72, f32[384,4096]{1,0:T(8,128)} %get-tuple-element.195, ...), kind=kLoop, calls=%fused_computation.113 | loop fusion | flops 25165824 | bytes 40894468 | tf_op jit(solution)/shard_map/broadcast_in_dim | solution.py:106
  (38 shorter events, 32.1 us)
Async XLA Ops:
  6.5 15.6 %copy-start = (bf16[12,128,896]{2,1,0:T(8,128)(2,1)S(1)}, bf16[12,128,896]{2,1,0:T(8,128)(2,1)}, u32[]{:S(2)}) copy-start(bf16[12,128,896]{2,1,0:T(8,128)(2,1)} %param.16) | copy-start | bytes 8257540
  6.5 297.3 %all-gather.2.cloned.1.call-start = ((), (), s32[]{:S(2)}) async-start(), calls=%async_computation.1 | async-start | bytes 17301504 | tf_op jit(solution)/shard_map/all_gather | solution.py:67
  14.1 289.7 %all-to-all-start = ((bf16[32,1,128,2048]{3,2,1,0:T(8,128)(2,1)}), bf16[32,1,128,2048]{3,2,1,0:T(8,128)(2,1)}, u32[]{:S(2)}, u32[]{:S(2)}) async-start(bf16[32,1,128,2048]{3,2,1,0:T(8,128)(2,1)} %stack.2), calls=%async_computation | async-start | bytes 33554432 | tf_op jit(solution)/shard_map/all_to_all | solution.py:65
  31.4 5.0 copy-start.4
  43.6 5.0 copy-start.2
  48.6 255.3 %copy-start.3 = (s32[1,12]{1,0:T(1,128)S(1)}, s32[1,12]{1,0:T(1,128)}, u32[]{:S(2)}) copy-start(s32[1,12]{1,0:T(1,128)} %param.17) | copy-start | bytes 148
  323.4 72.1 %collective-permute-start = (bf16[384,4096]{1,0:T(8,128)(2,1)}, bf16[384,4096]{1,0:T(8,128)(2,1)}, u32[]{:S(2)}, u32[]{:S(2)}) collective-permute-start(bf16[384,4096]{1,0:T(8,128)(2,1)} %broadcast_select_fusion), channel_id=1, source_target_pairs={{0,1},{1,2},{2,3},{4,5},{5,6},{6,7},{8,9},{9,10},{10,11},{12,13},{... | collective-permute-start | bytes 9437192 | tf_op jit(solution)/shard_map/ppermute | solution.py:18
  422.3 71.3 %collective-permute-start.1 = (bf16[384,4096]{1,0:T(8,128)(2,1)}, bf16[384,4096]{1,0:T(8,128)(2,1)}, u32[]{:S(2)}, u32[]{:S(2)}) collective-permute-start(bf16[384,4096]{1,0:T(8,128)(2,1)} %broadcast_select_fusion.1), channel_id=1, source_target_pairs={{0,1},{1,2},{2,3},{4,5},{5,6},{6,7},{8,9},{9,10},{10,11},{12,13},{... | collective-permute-start | bytes 9437192 | tf_op jit(solution)/shard_map/ppermute | solution.py:18
  520.5 244.6 %collective-permute-start.2 = (bf16[384,4096]{1,0:T(8,128)(2,1)}, bf16[384,4096]{1,0:T(8,128)(2,1)}, u32[]{:S(2)}, u32[]{:S(2)}) collective-permute-start(bf16[384,4096]{1,0:T(8,128)(2,1)} %broadcast_select_fusion.2), channel_id=1, source_target_pairs={{0,1},{1,2},{2,3},{4,5},{5,6},{6,7},{8,9},{9,10},{10,11},{12,13},{... | collective-permute-start | bytes 9437192 | tf_op jit(solution)/shard_map/ppermute | solution.py:18
  842.5 15.6 %copy-start.1 = (bf16[12,128,896]{2,1,0:T(8,128)(2,1)S(1)}, bf16[12,128,896]{2,1,0:T(8,128)(2,1)}, u32[]{:S(2)}) copy-start(bf16[12,128,896]{2,1,0:T(8,128)(2,1)} %param.16) | copy-start | bytes 8257540
Sparse Core Ops, SparseCore 0:
  9.5 266.1 all-gather.1
